TPU v7x, 256 devices: a whole 4x4x8 slice. The times are simulated.
256 devices in a mesh: gx: 64 (over z, x, core), gy: 4 (over y).
Axes of the slice: x: 4, y: 4, z: 8, core: 2. Of those that a mesh axis runs over, the one named last changes fastest.
Arguments:
- adjoint_block: float32 [4, 3, 64, 256, 512], P(None, None, None, 'gx', 'gy'), may hold values from -18 to 18
- base_flow: float32 [2, 3, 64, 256, 512], P(None, None, None, 'gx', 'gy'), may hold values from -4 to 4
- direct_modes: float32 [8, 3, 64, 256, 512], P(None, None, None, 'gx', 'gy'), may hold values from -0.0012207031 to 0.0012207031
- dual_modes: float32 [8, 3, 64, 256, 512], P(None, None, None, 'gx', 'gy'), may hold values from -0.6 to 0.6
Outputs:
- next_block: float32 [4, 3, 64, 256, 512], P(None, None, None, 'gx', 'gy')
- growth: float32 [4, 4], replicated
All inputs are finite; a program needn't handle non-finite values.
Results may differ from a plain program's by a relative error of at most 0.0001.
Values sent between devices are 32-bit elements; how exact they have to be, the bound alone decides.
A program may use at most 128 MiB of HBM per device.

v0:
```python
import math

import jax
import jax.numpy as jnp
from jax import lax
from jax.sharding import PartitionSpec as P

step_size = 0.1
viscosity = 0.2


def padded_2(shard, sides, width):
    for axis, dim in sides:
        count, length = (lax.axis_size(axis), shard.shape[dim])
        up = [(i, (i + 1) % count) for i in range(count - 1)]
        down = [(j, i) for i, j in up]
        last = lax.slice_in_dim(shard, length - width, length, axis=dim)
        leading = lax.slice_in_dim(shard, 0, width, axis=dim)
        before = lax.ppermute(last, axis, up)
        after = lax.ppermute(leading, axis, down)
        shard = jnp.concatenate([before, shard, after], axis=dim)
    return shard


def central_x(padded):
    return 0.5 * (padded[..., 2:, 1:-1] - padded[..., :-2, 1:-1])


def central_y(padded):
    return 0.5 * (padded[..., 1:-1, 2:] - padded[..., 1:-1, :-2])


def central_z(interior):
    return 0.5 * (jnp.roll(interior, -1, axis=-3) - jnp.roll(interior, 1, axis=-3))


def laplace(padded):
    interior = padded[..., 1:-1, 1:-1]
    beside_all = (
        padded[..., 2:, 1:-1]
        + padded[..., :-2, 1:-1]
        + padded[..., 1:-1, 2:]
        + padded[..., 1:-1, :-2]
    )
    beside_all = beside_all + jnp.roll(interior, -1, axis=-3) + jnp.roll(interior, 1, axis=-3)
    return beside_all - 6.0 * interior


def base_terms(padded_base):
    centre = padded_base[..., 1:-1, 1:-1]
    gradients = jnp.stack([central_x(padded_base), central_y(padded_base), central_z(centre)])
    return (centre, gradients)


def adjoint_step(padded, centre, gradients):
    interior = padded[..., 1:-1, 1:-1]
    advect = (
        centre[0] * central_x(padded)
        + centre[1] * central_y(padded)
        + centre[2] * central_z(interior)
    )
    produce = jnp.sum(interior[:, None] * gradients[None], axis=2)
    return interior + step_size * (advect - produce + viscosity * laplace(padded))


def project(left, right):
    return lax.dot_general(
        left,
        right,
        (((1,), (1,)), ((), ())),
        precision=lax.Precision.HIGHEST,
        preferred_element_type=jnp.float32,
    )


def combine_modes(coefficients, modes):
    return jnp.dot(
        coefficients.T, modes, precision=lax.Precision.HIGHEST, preferred_element_type=jnp.float32
    )


def extend_vectors(field):
    vectors, comps, depth, width_x, width_y = field.shape
    merged = field.reshape(vectors * comps, depth, width_x, width_y)
    padded = padded_2(merged, (("gx", 2), ("gy", 3)), 1)
    return padded.reshape(vectors, comps, depth, width_x + 2, width_y + 2)


def body(adjoint_block, base_flow, direct_modes, dual_modes):
    vectors, comps, depth, width_x, width_y = adjoint_block.shape
    mode_count = direct_modes.shape[0]
    row_count = comps * depth * width_x * width_y
    cell_total = float(
        comps * depth * width_x * lax.axis_size("gx") * width_y * lax.axis_size("gy")
    )
    padded_base = padded_2(
        base_flow.reshape(2 * comps, depth, width_x, width_y), (("gx", 2), ("gy", 3)), 1
    )
    padded_base = padded_base.reshape(2, comps, depth, width_x + 2, width_y + 2)
    direct_flat = direct_modes.reshape(mode_count, row_count)
    dual_flat = dual_modes.reshape(mode_count, row_count)
    padded = extend_vectors(adjoint_block)
    for substep in range(2):
        centre, gradients = base_terms(padded_base[substep])
        advanced = adjoint_step(padded, centre, gradients)
        flattened = advanced.reshape(vectors, row_count)
        partial_terms = project(direct_flat, flattened)
        coefficients = lax.psum(partial_terms, ("gx", "gy"))
        deflated = flattened - combine_modes(coefficients, dual_flat)
        if substep == 0:
            padded = extend_vectors(deflated.reshape(advanced.shape))
    gram_matrix = lax.psum(project(deflated, deflated), ("gx", "gy"))
    cholesky_factor = jnp.linalg.cholesky(gram_matrix)
    solved = jax.scipy.linalg.solve_triangular(cholesky_factor, deflated, lower=True)
    next_block = (math.sqrt(cell_total) * solved).reshape(adjoint_block.shape)
    return (next_block, cholesky_factor)


def solution(mesh):
    placed = (
        P(None, None, None, "gx", "gy"),
        P(None, None, None, "gx", "gy"),
        P(None, None, None, "gx", "gy"),
        P(None, None, None, "gx", "gy"),
    )
    return jax.shard_map(
        body,
        mesh=mesh,
        in_specs=placed,
        out_specs=(P(None, None, None, "gx", "gy"), P()),
        check_vma=False,
    )
```

profile of v0, /device:TPU:1, one launch (start us, length us, event | category | flops | bytes accessed | tf_op | source)
XLA Modules:
  0.0 437.2 jit_solution(15457875989147088941)
XLA Ops:
  0.6 2.9 copy.146
  3.5 2.2 fusion.43
  5.7 5.1 %collective-permute-start.4 = (f32[6,64,1,128]{1,3,2,0:T(8,128)}, f32[6,64,1,128]{1,3,2,0:T(8,128)S(1)}, u32[]{:S(2)}, u32[]{:S(2)}) collective-permute-start(f32[6,64,1,128]{1,3,2,0:T(8,128)} %get-tuple-element.41), channel_id=1, source_target_pairs={{4,0},{8,4},{12,8},{16,12},{20,16},{24,20},{28,24},{32,28},{36,32}... | collective-permute-start | bytes 589832 | tf_op jit(solution)/shard_map/ppermute | solution.py:20
  15.2 3.1 collective-permute-start.1
  18.3 2.4 collective-permute-start
  20.7 2.3 slice_bitcast_fusion.5
  23.0 2.1 slice_bitcast_fusion.4
  31.4 5.1 %reshape.186 = f32[8,98304]{1,0:T(8,128)} reshape(f32[8,3,64,4,128]{4,3,2,1,0:T(4,128)} %param.7) | data formatting | bytes 6291456 | tf_op jit(solution)/shard_map/reshape | solution.py:101
  36.5 4.9 %fusion.26 = (f32[1,3,64,4,128]{2,4,3,1,0:T(8,128)}, f32[1,3,64,4,128]{2,4,3,1,0:T(8,128)}) fusion(f32[1,3,1,4,128]{2,4,3,1,0:T(8,128)} %get-tuple-element.35, f32[1,3,63,4,128]{2,4,3,1,0:T(8,128)} %get-tuple-element.39, f32[1,3,63,4,128]{2,4,3,1,0:T(8,128)} %get-tuple-element.36, f32[1,3,1,4,128]{2,4,3,1,0:T(8,128)} %get-tuple-element.32, ...), kind=kLoop, calls=%fused_computation.53 | loop fusion | flops 786432 | bytes 2359296 | tf_op jit(solution)/shard_map/mul | solution.py:34
  42.3 2.6 collective-permute-start.7
  46.1 2.4 fusion.25
  52.2 3.1 fusion.40
  55.4 2.4 copy.143
  59.1 2.4 copy.142
  61.5 4.5 %collective-permute-start.2 = (f32[12,64,6,1]{1,3,2,0:T(1,128)S(1)}, f32[12,64,6,1]{1,3,2,0:T(1,128)S(1)}, u32[]{:S(2)}, u32[]{:S(2)}) collective-permute-start(f32[12,64,6,1]{1,3,2,0:T(1,128)S(1)} %copy.142), channel_id=1, source_target_pairs={{0,1},{1,2},{2,3},{4,5},{5,6},{6,7},{8,9},{9,10},{10,11},{12,13},{... | collective-permute-start | bytes 55304 | tf_op jit(solution)/shard_map/ppermute | solution.py:19
  66.0 3.3 pad_maximum_fusion.3
  69.3 2.8 copy.152
  72.2 2.2 copy.145
  74.4 2.2 copy.144
  76.6 4.9 %pad_maximum_fusion.1 = f32[12,64,6,130]{3,1,2,0:T(8,128)S(1)} fusion(f32[12,64,6,1]{3,1,2,0:T(8,128)} %copy.145, f32[12,64,1,128]{3,1,2,0:T(8,128)} %collective-permute-done.1, f32[12,64,4,128]{3,1,2,0:T(8,128)} %bitcast.87, f32[12,64,1,128]{3,1,2,0:T(8,128)} %collective-permute-done, f32[12,64,6,1]{3,1,2,0:T(8,128)} %copy.144), kind=kLoop, calls=%fused_computation.4 | loop fusion | flops 2396160 | bytes 4792320 | tf_op jit(solution)/shard_map/concatenate | solution.py:21
  86.3 2.2 copy.153
  88.5 8.9 %fusion.6 = f32[8,4]{0,1:T(4,128)S(1)} fusion(f32[8,3,64,4,128]{4,3,2,1,0:T(4,128)S(1)} %copy-done, f32[4,3,64,4,128]{4,2,3,1,0:T(8,128)S(1)} %multiply_add_fusion.1), kind=kOutput, calls=%fused_computation.22 | convolution fusion | flops 37748736 | bytes 4718720 | tf_op jit(solution)/shard_map/dot_general | solution.py:67
  97.4 3.6 reshape.185
  101.1 83.8 %psum.21 = f32[8,4]{0,1:T(4,128)S(1)} all-reduce(f32[8,4]{0,1:T(4,128)S(1)} %fusion.6), channel_id=1, replica_groups=mesh['gx'=64,'gy'=4] {'gx','gy'}, use_global_device_ids=true, to_apply=%region_1.2 | all-reduce | flops 32 | bytes 256 | tf_op jit(solution)/shard_map/psum | solution.py:108
  184.9 6.2 %convolution_subtract_fusion.1 = f32[4,98304]{1,0:T(4,128)} fusion(f32[4,98304]{1,0:T(4,128)} %reshape.185, f32[8,4]{0,1:T(4,128)S(1)} %psum.21, f32[8,98304]{1,0:T(8,128)} %reshape.186), kind=kOutput, calls=%fused_computation.2 | convolution fusion | flops 38141952 | bytes 6291584 | tf_op jit(solution)/shard_map/dot_general | solution.py:77
  191.1 3.9 reshape_reshape.3
  195.0 3.6 fusion.41
  198.7 2.6 collective-permute-start.9
  201.3 3.0 collective-permute-start.8
  207.8 3.3 copy.159
  211.1 2.2 copy.160
  213.3 2.2 copy.158
  218.1 4.0 collective-permute-start.10
  223.7 2.8 copy.167
  226.6 4.3 pad_maximum_fusion
  230.8 6.3 %copy.161 = f32[12,64,6,130]{3,1,2,0:T(8,128)} copy(f32[12,64,6,130]{1,3,2,0:T(8,128)} %pad_maximum_fusion) | data formatting | bytes 4792320 | tf_op jit(solution)/shard_map/concatenate | solution.py:21
  237.2 2.4 slice.360
  239.5 3.9 fusion.36
  245.0 2.3 multiply_add_fusion
  247.4 2.2 copy.168
  249.5 8.9 %fusion.11 = f32[8,4]{0,1:T(4,128)S(1)} fusion(f32[8,3,64,4,128]{4,3,2,1,0:T(4,128)S(1)} %copy-done, f32[4,3,64,4,128]{4,2,3,1,0:T(8,128)S(1)} %multiply_add_fusion), kind=kOutput, calls=%fused_computation.23 | convolution fusion | flops 37748736 | bytes 4718720 | tf_op jit(solution)/shard_map/dot_general | solution.py:67
  258.5 3.6 reshape.188
  262.1 75.8 %psum.22 = f32[8,4]{0,1:T(4,128)S(1)} all-reduce(f32[8,4]{0,1:T(4,128)S(1)} %fusion.11), channel_id=1, replica_groups=mesh['gx'=64,'gy'=4] {'gx','gy'}, use_global_device_ids=true, to_apply=%region_3.4 | all-reduce | flops 32 | bytes 256 | tf_op jit(solution)/shard_map/psum | solution.py:108
  337.9 5.1 %convolution_subtract_fusion = f32[4,98304]{1,0:T(4,128)S(1)} fusion(f32[4,98304]{1,0:T(4,128)} %reshape.188, f32[8,4]{0,1:T(4,128)S(1)} %psum.22, f32[8,98304]{1,0:T(8,128)} %reshape.186), kind=kOutput, calls=%fused_computation.1 | convolution fusion | flops 38141952 | bytes 6291584 | tf_op jit(solution)/shard_map/dot_general | solution.py:77
  344.2 6.8 %fusion.44 = f32[4,4]{0,1:T(4,128)S(1)} fusion(f32[4,98304]{1,0:T(4,128)S(1)} %convolution_subtract_fusion), kind=kOutput, calls=%fused_computation.91 | convolution fusion | flops 18874368 | bytes 1572928 | tf_op jit(solution)/shard_map/dot_general | solution.py:67
  351.0 73.8 %psum.23 = f32[4,4]{0,1:T(4,128)S(1)} all-reduce(f32[4,4]{0,1:T(4,128)S(1)} %fusion.44), channel_id=1, replica_groups=mesh['gx'=64,'gy'=4] {'gx','gy'}, use_global_device_ids=true, to_apply=%region_4.5 | all-reduce | flops 16 | bytes 128 | tf_op jit(solution)/shard_map/psum | solution.py:112
  427.6 5.5 %convolution_multiply_fusion = f32[4,98304]{1,0:T(4,128)} fusion(f32[4,98304]{1,0:T(4,128)} %copy-done.4, f32[1,4,4]{1,2,0:T(4,128)S(1)} %custom-call.7), kind=kOutput, calls=%fused_computation | convolution fusion | flops 19267584 | bytes 3145792 | tf_op jit(solution)/shard_map/jit(_solve_triangular)/triangular_solve | solution.py:114
  433.1 3.9 reshape.189
  (82 shorter events, 35.9 us)
Async XLA Ops:
  0.6 87.9 %copy-start = (f32[8,3,64,4,128]{4,3,2,1,0:T(4,128)S(1)}, f32[8,3,64,4,128]{4,3,2,1,0:T(4,128)}, u32[]{:S(2)}) copy-start(f32[8,3,64,4,128]{4,3,2,1,0:T(4,128)} %param.6) | copy-start | bytes 9437188
  3.5 9.2 %copy-start.12 = (f32[4,3,64,4,128]{4,3,2,1,0:T(4,128)S(1)}, f32[4,3,64,4,128]{4,3,2,1,0:T(4,128)}, u32[]{:S(2)}) copy-start(f32[4,3,64,4,128]{4,3,2,1,0:T(4,128)} %param.4) | copy-start | bytes 4718596
  5.7 35.7 %collective-permute-start.4 = (f32[6,64,1,128]{1,3,2,0:T(8,128)}, f32[6,64,1,128]{1,3,2,0:T(8,128)S(1)}, u32[]{:S(2)}, u32[]{:S(2)}) collective-permute-start(f32[6,64,1,128]{1,3,2,0:T(8,128)} %get-tuple-element.41), channel_id=1, source_target_pairs={{4,0},{8,4},{12,8},{16,12},{20,16},{24,20},{28,24},{32,28},{36,32}... | collective-permute-start | bytes 589832 | tf_op jit(solution)/shard_map/ppermute | solution.py:20
  10.9 30.6 %collective-permute-start.5 = (f32[6,64,1,128]{1,3,2,0:T(8,128)}, f32[6,64,1,128]{1,3,2,0:T(8,128)}, u32[]{:S(2)}, u32[]{:S(2)}) collective-permute-start(f32[6,64,1,128]{1,3,2,0:T(8,128)} %get-tuple-element.40), channel_id=1, source_target_pairs={{0,4},{4,8},{8,12},{12,16},{16,20},{20,24},{24,28},{28,32},{32,36}... | collective-permute-start | bytes 589832 | tf_op jit(solution)/shard_map/ppermute | solution.py:19
  13.0 1.2 copy-start.5
  13.0 7.7 %copy-start.1 = (f32[2,3,64,4,128]{2,4,3,1,0:T(8,128)S(1)}, f32[2,3,64,4,128]{2,4,3,1,0:T(8,128)}, u32[]{:S(2)}) copy-start(f32[2,3,64,4,128]{2,4,3,1,0:T(8,128)} %copy.146) | copy-start | bytes 2359300
  15.2 35.7 %collective-permute-start.1 = (f32[12,64,1,128]{3,1,2,0:T(8,128)}, f32[12,64,1,128]{3,1,2,0:T(8,128)}, u32[]{:S(2)}, u32[]{:S(2)}) collective-permute-start(f32[12,64,1,128]{3,1,2,0:T(8,128)} %get-tuple-element.31), channel_id=1, source_target_pairs={{4,0},{8,4},{12,8},{16,12},{20,16},{24,20},{28,24},{32,28},{36,32}... | collective-permute-start | bytes 1179656 | tf_op jit(solution)/shard_map/ppermute | solution.py:20
  18.3 32.6 %collective-permute-start = (f32[12,64,1,128]{3,1,2,0:T(8,128)}, f32[12,64,1,128]{3,1,2,0:T(8,128)}, u32[]{:S(2)}, u32[]{:S(2)}) collective-permute-start(f32[12,64,1,128]{3,1,2,0:T(8,128)} %get-tuple-element.30), channel_id=1, source_target_pairs={{0,4},{4,8},{8,12},{12,16},{16,20},{20,24},{24,28},{28,32},{32,36}... | collective-permute-start | bytes 1179656 | tf_op jit(solution)/shard_map/ppermute | solution.py:19
  36.5 4.9 %copy-start.2 = (f32[2,3,64,4,128]{2,4,3,1,0:T(8,128)S(1)}, f32[2,3,64,4,128]{2,4,3,1,0:T(8,128)}, u32[]{:S(2)}) copy-start(f32[2,3,64,4,128]{2,4,3,1,0:T(8,128)} %copy.146) | copy-start | bytes 2359300
  42.3 6.3 %collective-permute-start.7 = (f32[6,64,6,1]{1,3,2,0:T(1,128)S(1)}, f32[6,64,6,1]{1,3,2,0:T(1,128)S(1)}, u32[]{:S(2)}, u32[]{:S(2)}) collective-permute-start(f32[6,64,6,1]{1,3,2,0:T(1,128)S(1)} %get-tuple-element.21), channel_id=1, source_target_pairs={{0,1},{1,2},{2,3},{4,5},{5,6},{6,7},{8,9},{9,10},{10,11},{12,13},{... | collective-permute-start | bytes 27656 | tf_op jit(solution)/shard_map/ppermute | solution.py:19
  44.8 4.5 %collective-permute-start.6 = (f32[6,64,6,1]{1,3,2,0:T(1,128)S(1)}, f32[6,64,6,1]{1,3,2,0:T(1,128)S(1)}, u32[]{:S(2)}, u32[]{:S(2)}) collective-permute-start(f32[6,64,6,1]{1,3,2,0:T(1,128)S(1)} %get-tuple-element.20), channel_id=1, source_target_pairs={{1,0},{2,1},{3,2},{5,4},{6,5},{7,6},{9,8},{10,9},{11,10},{13,12},{... | collective-permute-start | bytes 27656 | tf_op jit(solution)/shard_map/ppermute | solution.py:20
  48.5 2.4 copy-start.6
  57.8 14.4 %collective-permute-start.3 = (f32[12,64,6,1]{1,3,2,0:T(1,128)S(1)}, f32[12,64,6,1]{1,3,2,0:T(1,128)S(1)}, u32[]{:S(2)}, u32[]{:S(2)}) collective-permute-start(f32[12,64,6,1]{1,3,2,0:T(1,128)S(1)} %copy.143), channel_id=1, source_target_pairs={{1,0},{2,1},{3,2},{5,4},{6,5},{7,6},{9,8},{10,9},{11,10},{13,12},{... | collective-permute-start | bytes 55304 | tf_op jit(solution)/shard_map/ppermute | solution.py:20
  61.5 12.9 %collective-permute-start.2 = (f32[12,64,6,1]{1,3,2,0:T(1,128)S(1)}, f32[12,64,6,1]{1,3,2,0:T(1,128)S(1)}, u32[]{:S(2)}, u32[]{:S(2)}) collective-permute-start(f32[12,64,6,1]{1,3,2,0:T(1,128)S(1)} %copy.142), channel_id=1, source_target_pairs={{0,1},{1,2},{2,3},{4,5},{5,6},{6,7},{8,9},{9,10},{10,11},{12,13},{... | collective-permute-start | bytes 55304 | tf_op jit(solution)/shard_map/ppermute | solution.py:19
  81.9 1.3 copy-start.7
  83.2 0.9 copy-start.14
  83.2 1.0 copy-start.15
  83.2 1.0 copy-start.16
  195.0 12.0 %copy-start.13 = (f32[64,4,128]{0,2,1:T(8,128)S(1)}, f32[64,4,128]{0,2,1:T(8,128)}, u32[]{:S(2)}) copy-start(f32[64,4,128]{0,2,1:T(8,128)} %get-tuple-element.22) | copy-start | bytes 393220
  198.7 12.4 %collective-permute-start.9 = (f32[12,64,1,128]{3,1,2,0:T(8,128)}, f32[12,64,1,128]{3,1,2,0:T(8,128)}, u32[]{:S(2)}, u32[]{:S(2)}) collective-permute-start(f32[12,64,1,128]{3,1,2,0:T(8,128)} %bitcast.36), channel_id=1, source_target_pairs={{4,0},{8,4},{12,8},{16,12},{20,16},{24,20},{28,24},{32,28},{36,32}... | collective-permute-start | bytes 1179656 | tf_op jit(solution)/shard_map/ppermute | solution.py:20
  201.3 12.1 %collective-permute-start.8 = (f32[12,64,1,128]{3,1,2,0:T(8,128)}, f32[12,64,1,128]{3,1,2,0:T(8,128)}, u32[]{:S(2)}, u32[]{:S(2)}) collective-permute-start(f32[12,64,1,128]{3,1,2,0:T(8,128)} %bitcast.35), channel_id=1, source_target_pairs={{0,4},{4,8},{8,12},{12,16},{16,20},{20,24},{24,28},{28,32},{32,36}... | collective-permute-start | bytes 1179656 | tf_op jit(solution)/shard_map/ppermute | solution.py:19
  215.5 6.6 %copy-start.9 = (f32[1,3,64,4,128]{2,4,3,1,0:T(8,128)S(1)}, f32[1,3,64,4,128]{2,4,3,1,0:T(8,128)}, u32[]{:S(2)}) copy-start(f32[1,3,64,4,128]{2,4,3,1,0:T(8,128)} %get-tuple-element.15) | copy-start | bytes 1179652
  215.5 6.6 %copy-start.10 = (f32[1,3,64,4,128]{2,4,3,1,0:T(8,128)S(1)}, f32[1,3,64,4,128]{2,4,3,1,0:T(8,128)}, u32[]{:S(2)}) copy-start(f32[1,3,64,4,128]{2,4,3,1,0:T(8,128)} %get-tuple-element.19) | copy-start | bytes 1179652
  215.5 6.6 %copy-start.11 = (f32[1,3,64,4,128]{2,4,3,1,0:T(8,128)S(1)}, f32[1,3,64,4,128]{2,4,3,1,0:T(8,128)}, u32[]{:S(2)}) copy-start(f32[1,3,64,4,128]{2,4,3,1,0:T(8,128)} %get-tuple-element.43) | copy-start | bytes 1179652
  216.8 9.8 %collective-permute-start.11 = (f32[12,64,6,1]{1,3,2,0:T(1,128)S(1)}, f32[12,64,6,1]{1,3,2,0:T(1,128)S(1)}, u32[]{:S(2)}, u32[]{:S(2)}) collective-permute-start(f32[12,64,6,1]{1,3,2,0:T(1,128)S(1)} %get-tuple-element.9), channel_id=1, source_target_pairs={{1,0},{2,1},{3,2},{5,4},{6,5},{7,6},{9,8},{10,9},{11,10},{13,12},{... | collective-permute-start | bytes 55304 | tf_op jit(solution)/shard_map/ppermute | solution.py:20
  218.1 8.5 %collective-permute-start.10 = (f32[12,64,6,1]{1,3,2,0:T(1,128)S(1)}, f32[12,64,6,1]{1,3,2,0:T(1,128)S(1)}, u32[]{:S(2)}, u32[]{:S(2)}) collective-permute-start(f32[12,64,6,1]{1,3,2,0:T(1,128)S(1)} %get-tuple-element.8), channel_id=1, source_target_pairs={{0,1},{1,2},{2,3},{4,5},{5,6},{6,7},{8,9},{9,10},{10,11},{12,13},{... | collective-permute-start | bytes 55304 | tf_op jit(solution)/shard_map/ppermute | solution.py:19
  239.5 4.2 copy-start.3
  239.5 4.5 %copy-start.8 = (f32[3,3,64,4,128]{4,2,3,1,0:T(8,128)S(1)}, f32[3,3,64,4,128]{4,2,3,1,0:T(8,128)}, u32[]{:S(2)}) copy-start(f32[3,3,64,4,128]{4,2,3,1,0:T(8,128)} %copy.167) | copy-start | bytes 3538948
  244.1 0.9 copy-start.17
  244.1 1.0 copy-start.18
  343.0 1.1 copy-start.4
where the time goes:
time: 444 us; the launch traced here: 437 us
  blocking collectives  233 us (52%)
  local copies, waits for them, and re-layouts  91.6 us (21%)
  matrix products  41.5 us (9%)
  other arithmetic  35.5 us (8%)
  starting transfers between devices  33.1 us (7%)
    psum x2, blocking collectives, body(): coefficients = lax.psum(partial_terms, ('gx', 'gy'))  160 us
    psum x1, blocking collectives, body(): gram_matrix = lax.psum(project(deflated, deflated), ('gx', 'gy'))  73.8 us
    dot_general x3, matrix products, project(): lax.dot_general(left, right, (((1,), (1,)), ((), ())), precision=lax.Prec...  24.7 us
    ppermute x6, starting transfers between devices, padded_2(): before = lax.ppermute(last, axis, up)  18.4 us
    ppermute x6, starting transfers between devices, padded_2(): after = lax.ppermute(leading, axis, down)  14.7 us
    slice x5, local copies, waits for them, and re-layouts, padded_2(): last = lax.slice_in_dim(shard, length - width, length, axis=dim)  12.3 us
    dot_general x2, matrix products, combine_modes(): jnp.dot(coefficients.T, modes, precision=lax.Precision.HIGHEST, preferred...  11.3 us
    concatenate x3, other arithmetic, padded_2(): shard = jnp.concatenate([before, shard, after], axis=dim)  10.5 us
  transfers between devices with their start and end apart: 12, of which 1 were waited for; matrix products, arithmetic and copies ran while one was open for 12% of the time, Pallas kernels for 0%

commit v1 on v0

v1 whole, which is shorter than its diff:
```python
import functools
import math

import jax
import jax.numpy as jnp
from jax import lax
from jax.experimental import pallas as pl
from jax.experimental.pallas import tpu as pltpu
from jax.sharding import PartitionSpec as P

MESH = pl.DeviceIdType.MESH
F32 = jnp.float32
STEP = 0.1
VISC = 0.2
V, C, M = 4, 3, 8
XL, LN = 4, 128
CHIPS_X = 4
PAIRS_C = 32
PAIRS_FF = 32
PAIRS_UF = 42
PAIRS_UU = 74
PAIRS = 110


def kernel(
    n_gx, n_gy, nz, cells,
    q_hbm, b_hbm, d_hbm, u_hbm, out_hbm, growth_ref,
    q, b, d, u, a1, q1, f, out,
    xs, xr, bxs, bxr, ys, yr, bys, byr, w, wb,
    acc, ca, cb, coef, g1a, g1b, g2a, g2b,
    in_sem, out_sem, sx_sem, rx_sem, sy_sem, ry_sem, sg_sem, rg_sem,
):
    rows = nz * XL
    blocks = nz // 8
    nf = V * C
    gx, gy = lax.axis_index("gx"), lax.axis_index("gy")
    core = lax.rem(gx, 2)
    cx = lax.rem(lax.div(gx, 2), CHIPS_X)
    cz = lax.div(gx, 2 * CHIPS_X)
    n_z = n_gx // (2 * CHIPS_X)
    size_a, size_b = 2 * n_z, CHIPS_X * n_gy
    me_a, me_b = cz * 2 + core, cx * n_gy + gy

    def member_a(i):
        return ((lax.div(i, 2) * CHIPS_X + cx) * 2 + lax.rem(i, 2), gy)

    def member_b(i):
        return ((cz * CHIPS_X + lax.div(i, n_gy)) * 2 + core, lax.rem(i, n_gy))

    left, right = (lax.rem(gx + n_gx - 1, n_gx), gy), (lax.rem(gx + 1, n_gx), gy)
    below, above = (gx, lax.rem(gy + n_gy - 1, n_gy)), (gx, lax.rem(gy + 1, n_gy))
    has_l, has_r = gx > 0, gx < n_gx - 1
    has_b, has_a = gy > 0, gy < n_gy - 1

    q_main = pltpu.make_async_copy(q_hbm, q.at[:, pl.ds(8, rows), :], in_sem.at[0])
    q_low = pltpu.make_async_copy(q_hbm.at[:, pl.ds(rows - 8, 8), :], q.at[:, pl.ds(0, 8), :], in_sem.at[1])
    q_high = pltpu.make_async_copy(q_hbm.at[:, pl.ds(0, 8), :], q.at[:, pl.ds(rows + 8, 8), :], in_sem.at[2])
    b_main = pltpu.make_async_copy(b_hbm, b.at[:, pl.ds(8, rows), :], in_sem.at[3])
    b_low = pltpu.make_async_copy(b_hbm.at[:, pl.ds(rows - 8, 8), :], b.at[:, pl.ds(0, 8), :], in_sem.at[4])
    b_high = pltpu.make_async_copy(b_hbm.at[:, pl.ds(0, 8), :], b.at[:, pl.ds(rows + 8, 8), :], in_sem.at[5])
    u_main = pltpu.make_async_copy(u_hbm, u, in_sem.at[6])
    d_main = pltpu.make_async_copy(d_hbm, d, in_sem.at[7])
    q_main.start()
    b_main.start()
    for copy in (q_low, q_high, b_low, b_high, u_main, d_main):
        copy.start()

    barrier = pltpu.get_barrier_semaphore()
    for peer in (left, right, below, above):
        pl.semaphore_signal(barrier, inc=1, device_id=peer, device_id_type=MESH)

    @pl.loop(1, size_a)
    def _(step):
        pl.semaphore_signal(
            barrier, inc=1, device_id=member_a(lax.rem(me_a + step, size_a)), device_id_type=MESH
        )

    @pl.loop(1, size_b)
    def _(step):
        pl.semaphore_signal(
            barrier, inc=1, device_id=member_b(lax.rem(me_b + step, size_b)), device_id_type=MESH
        )

    lane = lax.broadcasted_iota(jnp.int32, (8, LN), 1)
    half = lax.shift_right_logical(lane, 1)
    first, final, odd = lane == 0, lane == LN - 1, lax.rem(lane, 2) == 1

    def plane(ref, field, k, x, dz=0, pad=8):
        return ref[field, pl.ds(pad + 8 * XL * k + x + XL * dz, 8, stride=XL), :]

    def zero(ref, count):
        @pl.loop(0, count)
        def _(i):
            ref[i] = jnp.zeros((nz, LN), F32)

    def x_copy(send, recv, side, sem):
        peer = left if side == 0 else right
        return pltpu.make_async_remote_copy(
            src_ref=send.at[side], dst_ref=recv.at[1 - side],
            send_sem=sx_sem.at[sem + side], recv_sem=rx_sem.at[sem + 1 - side],
            device_id=peer, device_id_type=MESH,
        )

    def x_start(send, recv, sem):
        for side, there in ((0, has_l), (1, has_r)):
            @pl.when(there)
            def _():
                x_copy(send, recv, side, sem).start()

    def x_wait(send, recv, sem, count):
        for side, there in ((0, has_l), (1, has_r)):
            @pl.when(there)
            def _():
                x_copy(send, recv, 1 - side, sem).wait_recv()

    def x_sent(send, recv, sem):
        for side, there in ((0, has_l), (1, has_r)):
            @pl.when(there)
            def _():
                x_copy(send, recv, side, sem).wait_send()

    def x_zero(recv, count):
        for side, there in ((0, has_l), (1, has_r)):
            @pl.when(jnp.logical_not(there))
            def _():
                zero(recv.at[side], count)

    def y_copy(send, recv, side, sem):
        peer = below if side == 0 else above
        return pltpu.make_async_remote_copy(
            src_ref=send, dst_ref=recv.at[1 - side],
            send_sem=sy_sem.at[sem + side], recv_sem=ry_sem.at[sem + 1 - side],
            device_id=peer, device_id_type=MESH,
        )

    def y_start(send, recv, sem):
        for side, there in ((0, has_b), (1, has_a)):
            @pl.when(there)
            def _():
                y_copy(send, recv, side, sem).start()

    def y_wait(send, recv, sem):
        for side, there in ((0, has_b), (1, has_a)):
            @pl.when(there)
            def _():
                y_copy(send, recv, 1 - side, sem).wait_recv()

    def y_sent(send, recv, sem):
        for side, there in ((0, has_b), (1, has_a)):
            @pl.when(there)
            def _():
                y_copy(send, recv, side, sem).wait_send()

    def y_zero(recv):
        for side, there in ((0, has_b), (1, has_a)):
            @pl.when(jnp.logical_not(there))
            def _():
                recv[side] = jnp.zeros((nz, LN), F32)

    def x_pack(ref, send, count):
        @pl.loop(0, count)
        def _(i):
            for k in range(blocks):
                at = pl.ds(8 * k, 8)
                send[0, i, at, :] = plane(ref, i, k, 0)
                send[1, i, at, :] = plane(ref, i, k, XL - 1)

    def y_pack(ref, send, count):
        @pl.loop(0, blocks)
        def _(k):
            total = jnp.zeros((8, LN), F32)
            for x in range(XL):
                for i in range(count):
                    at = 16 * x + i
                    total = jnp.where(half == at, pltpu.roll(plane(ref, i, k, x), 2 * at + 1, 1), total)
            send[pl.ds(pl.multiple_of(8 * k, 8), 8), :] = total

    def y_merge(recv, merged):
        for k in range(blocks):
            at = pl.ds(8 * k, 8)
            merged[at, :] = jnp.where(
                odd, pltpu.roll(recv[0, at, :], 1, 1), pltpu.roll(recv[1, at, :], LN - 1, 1)
            )

    def beside_y(value, edges, x, field):
        fix = pltpu.roll(edges, LN - (32 * x + 2 * field + 1), 1)
        return (
            jnp.where(first, fix, pltpu.roll(value, 1, 1)),
            jnp.where(final, fix, pltpu.roll(value, LN - 1, 1)),
        )

    def beside_x(ref, recv, field, k, x):
        at = pl.ds(pl.multiple_of(8 * k, 8), 8)
        low = recv[0, field, at, :] if x == 0 else plane(ref, field, k, x - 1)
        high = recv[1, field, at, :] if x == XL - 1 else plane(ref, field, k, x + 1)
        return low, high

    def stencil(src, src_x, edges, s, dst, planes):
        @pl.loop(0, blocks)
        def _(k):
            at = pl.ds(pl.multiple_of(8 * k, 8), 8)
            wk, wbk = edges[at, :], wb[at, :]
            for x in planes:
                base = [plane(b, 3 * s + j, k, x) for j in range(C)]
                low = [VISC * STEP - 0.5 * STEP * t for t in base]
                high = [VISC * STEP + 0.5 * STEP * t for t in base]
                mix = [[None] * C for _ in range(C)]
                for j in range(C):
                    field = 3 * s + j
                    xm, xp = beside_x(b, bxr, field, k, x)
                    ym, yp = beside_y(base[j], wbk, x, field)
                    zm, zp = plane(b, field, k, x, -1), plane(b, field, k, x, 1)
                    for c, (m_, p_) in enumerate(((xm, xp), (ym, yp), (zm, zp))):
                        mix[c][j] = 0.5 * STEP * (m_ - p_)
                for c in range(C):
                    mix[c][c] = mix[c][c] + (1.0 - 6.0 * VISC * STEP)
                for v in range(V):
                    mid = [plane(src, C * v + c, k, x) for c in range(C)]
                    for c in range(C):
                        field = C * v + c
                        xm, xp = beside_x(src, src_x, field, k, x)
                        ym, yp = beside_y(mid[c], wk, x, field)
                        zm, zp = plane(src, field, k, x, -1), plane(src, field, k, x, 1)
                        total = mix[c][0] * mid[0] + mix[c][1] * mid[1] + mix[c][2] * mid[2]
                        total = total + (low[0] * xm + high[0] * xp)
                        total = total + (low[1] * ym + high[1] * yp)
                        total = total + (low[2] * zm + high[2] * zp)
                        dst[field, pl.ds(8 * XL * k + x, 8, stride=XL), :] = total

    def pair_sums(start, pairs, loader):
        zeros = tuple(jnp.zeros((8, LN), F32) for _ in pairs)

        def body(t, sums):
            sums = list(sums)
            at = pl.ds(pl.multiple_of(8 * t, 8), 8)
            for c in range(C):
                left_, right_ = loader(c, at)
                for n, (i, j) in enumerate(pairs):
                    sums[n] = sums[n] + left_[i] * right_[j]
            return tuple(sums)

        sums = lax.fori_loop(0, rows // 8, body, zeros)
        for n, value in enumerate(sums):
            acc[pl.ds(start + n, 1), :] = jnp.sum(value, axis=0, keepdims=True)

    ones = jnp.ones((8, LN), F32)

    def all_reduce(part_a, part_b, row, which):
        def stage(buf, size, me, member, sem):
            def copy(i, peer):
                return pltpu.make_async_remote_copy(
                    src_ref=buf.at[i], dst_ref=buf.at[i],
                    send_sem=sg_sem.at[sem], recv_sem=rg_sem.at[sem],
                    device_id=peer, device_id_type=MESH,
                )

            @pl.loop(1, size)
            def _(step):
                copy(me, member(lax.rem(me + step, size))).start()

            everything = pltpu.make_async_remote_copy(
                src_ref=buf.at[pl.ds(0, size - 1)], dst_ref=buf.at[pl.ds(0, size - 1)],
                send_sem=sg_sem.at[sem], recv_sem=rg_sem.at[sem],
                device_id=member(lax.rem(me + 1, size)), device_id_type=MESH,
            )
            everything.wait_recv()
            everything.wait_send()
            total = buf[0]
            for i in range(1, size):
                total = total + buf[i]
            return total

        part_a[me_a] = row
        part_b[me_b] = stage(part_a, size_a, me_a, member_a, 2 * which)
        return stage(part_b, size_b, me_b, member_b, 2 * which + 1)

    def lane_sums():
        return lax.dot_general(
            ones, acc[...], (((1,), (1,)), ((), ())),
            precision=lax.Precision.HIGHEST, preferred_element_type=F32,
        )[0:1, :]

    def spread(row, count, dst):
        r = lax.broadcasted_iota(jnp.int32, (count, LN), 0)
        l = lax.broadcasted_iota(jnp.int32, (count, LN), 1)
        chosen = jnp.where(r == l, jnp.broadcast_to(row, (count, LN)), 0.0)
        dst[pl.ds(0, count), :] = lax.dot_general(
            chosen, jnp.ones((LN, LN), F32), (((1,), (0,)), ((), ())),
            precision=lax.Precision.HIGHEST, preferred_element_type=F32,
        )

    q_main.wait()
    x_pack(q, xs.at[0], nf)
    b_main.wait()
    x_pack(b, bxs, 2 * C)
    pl.semaphore_wait(barrier, 4 + (size_a - 1) + (size_b - 1))
    x_start(xs.at[0], xr.at[0], 0)
    y_pack(q, ys.at[0], nf)
    y_start(ys.at[0], yr.at[0], 0)
    x_start(bxs, bxr, 2)
    y_pack(b, bys, 2 * C)
    y_start(bys, byr, 2)
    x_zero(xr.at[0], nf)
    x_zero(xr.at[1], nf)
    x_zero(bxr, 2 * C)
    y_zero(yr.at[0])
    y_zero(yr.at[1])
    y_zero(byr)
    for copy in (q_low, q_high, b_low, b_high, u_main):
        copy.wait()

    acc[...] = jnp.zeros((LN, LN), F32)
    uu = [(i, j) for i in range(M) for j in range(i, M)]

    def load_uu(c, at):
        rows_ = [u[C * i + c, at, :] for i in range(M)]
        return rows_, rows_

    pair_sums(PAIRS_UU, uu, load_uu)

    y_wait(ys.at[0], yr.at[0], 0)
    y_wait(bys, byr, 2)
    y_merge(yr.at[0], w)
    y_merge(byr, wb)
    stencil(q, xr.at[0], w, 0, a1, (1, 2))
    x_wait(xs.at[0], xr.at[0], 0, nf)
    x_wait(bxs, bxr, 2, 2 * C)
    stencil(q, xr.at[0], w, 0, a1, (0, 3))
    d_main.wait()

    modes_by_vectors = [(m, i) for m in range(M) for i in range(V)]

    def load_da(field):
        def loader(c, at):
            return [d[C * m + c, at, :] for m in range(M)], [field[C * i + c, at, :] for i in range(V)]
        return loader

    pair_sums(0, modes_by_vectors, load_da(a1))
    row1 = all_reduce(g1a, g1b, lane_sums(), 0)
    spread(row1, PAIRS_C, ca)

    def deflate(planes, send):
        @pl.loop(0, blocks)
        def _(k):
            at = pl.ds(pl.multiple_of(8 * k, 8), 8)
            for c in range(C):
                for x in planes:
                    dual = [plane(u, C * m + c, k, x, 0, 0) for m in range(M)]
                    for i in range(V):
                        field = C * i + c
                        total = plane(a1, field, k, x, 0, 0)
                        for m in range(M):
                            total = total - ca[pl.ds(V * m + i, 1), :] * dual[m]
                        q1[field, pl.ds(8 + 8 * XL * k + x, 8, stride=XL), :] = total
                        if send:
                            xs[1, 0 if x == 0 else 1, field, at, :] = total

    deflate((0, 3), True)
    x_start(xs.at[1], xr.at[1], 4)
    deflate((1, 2), False)
    y_pack(q1, ys.at[1], nf)
    y_start(ys.at[1], yr.at[1], 4)
    for field in range(nf):
        q1[field, pl.ds(0, 8), :] = q1[field, pl.ds(rows, 8), :]
        q1[field, pl.ds(rows + 8, 8), :] = q1[field, pl.ds(8, 8), :]
    y_wait(ys.at[1], yr.at[1], 4)
    y_merge(yr.at[1], w)
    stencil(q1, xr.at[1], w, 1, f, (1, 2))
    x_wait(xs.at[1], xr.at[1], 4, nf)
    stencil(q1, xr.at[1], w, 1, f, (0, 3))

    pair_sums(0, modes_by_vectors, load_da(f))
    tri = [(i, j) for i in range(V) for j in range(i, V)]

    def load_f(c, at):
        both = [f[C * i + c, at, :] for i in range(V)]
        both = both + [u[C * m + c, at, :] for m in range(M)]
        return both, both

    pair_sums(PAIRS_FF, tri + [(V + m, i) for m in range(M) for i in range(V)], load_f)
    row2 = all_reduce(g2a, g2b, lane_sums(), 1)
    spread(row2, 112, cb)

    def val(n):
        return cb[pl.ds(n, 1), :]

    c2 = [[val(V * m + i) for i in range(V)] for m in range(M)]
    ff, uf, dd = {}, {}, {}
    for n, (i, j) in enumerate(tri):
        ff[i, j] = val(PAIRS_FF + n)
    for m in range(M):
        for i in range(V):
            uf[m, i] = val(PAIRS_UF + V * m + i)
    for n, (i, j) in enumerate(uu):
        dd[i, j] = dd[j, i] = val(PAIRS_UU + n)

    def total_of(terms):
        terms = list(terms)
        while len(terms) > 1:
            terms = [
                terms[i] + terms[i + 1] if i + 1 < len(terms) else terms[i] for i in range(0, len(terms), 2)
            ]
        return terms[0]

    gram = {}
    for j in range(V):
        h = [total_of(dd[m, n] * c2[n][j] for n in range(M)) - uf[m, j] for m in range(M)]
        for i in range(j, V):
            gram[i, j] = ff[j, i] + total_of(c2[m][i] * h[m] - c2[m][j] * uf[m, i] for m in range(M))
    low = {}
    inv = {}
    for j in range(V):
        pivot = gram[j, j]
        for k in range(j):
            pivot = pivot - low[j, k] * low[j, k]
        low[j, j] = jnp.sqrt(pivot)
        inv[j, j] = 1.0 / low[j, j]
        for i in range(j + 1, V):
            total = gram[i, j]
            for k in range(j):
                total = total - low[i, k] * low[j, k]
            low[i, j] = total * inv[j, j]
    for i in range(V):
        for j in range(i):
            total = low[i, j] * inv[j, j]
            for k in range(j + 1, i):
                total = total + low[i, k] * inv[k, j]
            inv[i, j] = -total * inv[i, i]
    lane1 = lax.broadcasted_iota(jnp.int32, (1, LN), 1)
    for i in range(V):
        row = jnp.zeros((1, LN), F32)
        for j in range(i + 1):
            row = jnp.where(lane1 == j, low[i, j], row)
        growth_ref[pl.ds(i, 1), :] = row[:, 0:V]
    scale = math.sqrt(cells)
    slot = {}
    n = 0
    for i in range(V):
        for j in range(i + 1):
            coef[pl.ds(n, 1), :] = scale * inv[i, j]
            slot["f", i, j] = n
            n += 1
    for i in range(V):
        for m in range(M):
            coef[pl.ds(n, 1), :] = -scale * total_of(inv[i, j] * c2[m][j] for j in range(i + 1))
            slot["u", i, m] = n
            n += 1

    for c in range(C):
        @pl.loop(0, rows // 8)
        def _(t):
            at = pl.ds(pl.multiple_of(8 * t, 8), 8)
            fs = [f[C * i + c, at, :] for i in range(V)]
            us = [u[C * m + c, at, :] for m in range(M)]
            for i in range(V):
                terms = [coef[pl.ds(slot["f", i, j], 1), :] * fs[j] for j in range(i + 1)]
                terms += [coef[pl.ds(slot["u", i, m], 1), :] * us[m] for m in range(M)]
                out[C * i + c, at, :] = total_of(terms)

        for i in range(V):
            pltpu.make_async_copy(out.at[C * i + c], out_hbm.at[C * i + c], out_sem.at[C * i + c]).start()
    for n in range(nf):
        pltpu.make_async_copy(out.at[n], out_hbm.at[n], out_sem.at[n]).wait()
    x_sent(xs.at[0], xr.at[0], 0)
    x_sent(bxs, bxr, 2)
    x_sent(xs.at[1], xr.at[1], 4)
    y_sent(ys.at[0], yr.at[0], 0)
    y_sent(bys, byr, 2)
    y_sent(ys.at[1], yr.at[1], 4)


def body(n_gx, n_gy, adjoint_block, base_flow, direct_modes, dual_modes):
    nz = adjoint_block.shape[2]
    rows = nz * XL
    cells = float(C * nz * XL * n_gx * LN * n_gy)
    nf = V * C
    size_a, size_b = 2 * (n_gx // (2 * CHIPS_X)), CHIPS_X * n_gy
    vm = lambda *shape: pltpu.VMEM(shape, F32)
    anyspace = pl.BlockSpec(memory_space=pltpu.HBM)
    out, growth = pl.pallas_call(
        functools.partial(kernel, n_gx, n_gy, nz, cells),
        name="adjoint_step",
        out_shape=(
            jax.ShapeDtypeStruct((nf, rows, LN), F32),
            jax.ShapeDtypeStruct((V, V), F32),
        ),
        in_specs=[anyspace] * 4,
        out_specs=(anyspace, pl.BlockSpec(memory_space=pltpu.VMEM)),
        scratch_shapes=[
            vm(nf, rows + 16, LN), vm(2 * C, rows + 16, LN), vm(M * C, rows, LN), vm(M * C, rows, LN),
            vm(nf, rows, LN), vm(nf, rows + 16, LN), vm(nf, rows, LN), vm(nf, rows, LN),
            vm(2, 2, nf, nz, LN), vm(2, 2, nf, nz, LN), vm(2, 2 * C, nz, LN), vm(2, 2 * C, nz, LN),
            vm(2, nz, LN), vm(2, 2, nz, LN), vm(nz, LN), vm(2, nz, LN), vm(nz, LN), vm(nz, LN),
            vm(LN, LN), vm(PAIRS_C, LN), vm(112, LN), vm(48, LN),
            vm(size_a, 1, LN), vm(size_b, 1, LN), vm(size_a, 1, LN), vm(size_b, 1, LN),
            pltpu.SemaphoreType.DMA((8,)), pltpu.SemaphoreType.DMA((nf,)),
            pltpu.SemaphoreType.DMA((6,)), pltpu.SemaphoreType.DMA((6,)),
            pltpu.SemaphoreType.DMA((6,)), pltpu.SemaphoreType.DMA((6,)),
            pltpu.SemaphoreType.DMA((4,)), pltpu.SemaphoreType.DMA((4,)),
        ],
        compiler_params=pltpu.CompilerParams(
            collective_id=0, has_side_effects=True, vmem_limit_bytes=48 * 1024 * 1024
        ),
    )(
        adjoint_block.reshape(nf, rows, LN),
        base_flow.reshape(2 * C, rows, LN),
        direct_modes.reshape(M * C, rows, LN),
        dual_modes.reshape(M * C, rows, LN),
    )
    return out.reshape(adjoint_block.shape), growth


def solution(mesh):
    spec = P(None, None, None, "gx", "gy")
    return jax.shard_map(
        functools.partial(body, mesh.shape["gx"], mesh.shape["gy"]),
        mesh=mesh,
        in_specs=(spec,) * 4,
        out_specs=(spec, P()),
        check_vma=False,
    )
```

time: 444 us -> 62.3 us (0.14); the launches traced: 437 us -> 62.1 us
  blocking collectives: 233 us -> 0 us
  local copies, waits for them, and re-layouts: 91.6 us -> 4.26 us
  Pallas kernels: 0 us -> 57.2 us
  matrix products: 41.5 us -> 0 us
  other arithmetic: 35.5 us -> 0 us
  starting transfers between devices: 33.1 us -> 0 us
    psum x3 -> x0, blocking collectives: 233 us -> none  [the longest x2 160 us: body(): coefficients = lax.psum(partial_terms, ('gx', 'gy'))]
    pallas_call x0 -> x1, Pallas kernels: none -> 57.2 us  [body(): pl.pallas_call(functools.partial(kernel, n_gx, n_gy, nz, cells), name='ad...]
    dot_general x5 -> x0, matrix products: 36 us -> none  [the longest x3 24.7 us: project(): lax.dot_general(left, right, (((1,), (1,)), ((), ())), precision=lax.Prec...]
    ppermute x12 -> x0, starting transfers between devices: 33.1 us -> none  [the longest x6 18.4 us: padded_2(): before = lax.ppermute(last, axis, up)]
    slice x12 -> x0, local copies, waits for them, and re-layouts: 22.6 us -> none  [the longest x5 12.3 us: padded_2(): last = lax.slice_in_dim(shard, length - width, length, axis=dim)]
    reshape x4 -> x0, local copies, waits for them, and re-layouts: 16.2 us -> none  [the longest x2 7.26 us: body(): flattened = advanced.reshape(vectors, row_count)]
    another operation x4 -> x0, local copies, waits for them, and re-layouts: 12.8 us -> none  [the longest x2 7.21 us: extend_vectors(): merged = field.reshape(vectors * comps, depth, width_x, width_y)]
    another operation x9 -> x0, other arithmetic: 11.6 us -> none  [the longest x4 8.88 us: base_terms(): jnp.stack([central_x(padded_base), central_y(padded_base), central_z(cent...]
  transfers between devices with their start and end apart: 12 -> 0, of which waited for: 1 -> 0; matrix products, arithmetic and copies ran while one was open for 12% -> 0% of each run, Pallas kernels for 0% -> 0%
where the time goes in v1:
time: 62.3 us; the launch traced here: 62.1 us
  Pallas kernels  57.2 us (92%)
  local copies, waits for them, and re-layouts  4.26 us (7%)
  between operations  0.65 us (1%)
    pallas_call x1, Pallas kernels, body(): pl.pallas_call(functools.partial(kernel, n_gx, n_gy, nz, cells), name='ad...  57.2 us
    unnamed x6, local copies, waits for them, and re-layouts  4.26 us

profile of v1, /device:TPU:1, one launch (start us, length us, event | category | flops | bytes accessed | tf_op | source)
XLA Modules:
  0.0 62.1 jit_solution(5689972208044952386)
XLA Ops:
  0.6 0.0 copy-start
  0.6 1.4 %copy-done = f32[4,3,64,4,128]{4,3,2,1,0:T(4,128)S(1)} copy-done((f32[4,3,64,4,128]{4,3,2,1,0:T(4,128)S(1)}, f32[4,3,64,4,128]{4,3,2,1,0:T(4,128)}, u32[]{:S(2)}) %copy-start) | copy-done | bytes 1572888
  2.0 0.0 copy-start.1
  2.0 1.1 %copy-done.1 = f32[2,3,64,4,128]{4,3,2,1,0:T(4,128)S(1)} copy-done((f32[2,3,64,4,128]{4,3,2,1,0:T(4,128)S(1)}, f32[2,3,64,4,128]{4,3,2,1,0:T(4,128)}, u32[]{:S(2)}) %copy-start.1) | copy-done | bytes 786456
  3.2 57.2 %adjoint_step.1 = (f32[12,256,128]{2,1,0:T(8,128)S(1)}, f32[4,4]{1,0:T(4,128)S(1)}) custom-call(f32[12,256,128]{2,1,0:T(8,128)S(1)} %bitcast.6, f32[6,256,128]{2,1,0:T(8,128)S(1)} %bitcast.7, f32[24,256,128]{2,1,0:T(8,128)} %bitcast.8, f32[24,256,128]{2,1,0:T(8,128)} %bitcast.9), custom_call_target="tpu_custom_call" | custom-call | tf_op jit(solution)/shard_map/adjoint_step/pallas_call | solution.py:480
  60.4 1.1 %copy.8 = f32[4,3,64,4,128]{4,3,2,1,0:T(4,128)} copy(f32[4,3,64,4,128]{4,3,2,1,0:T(4,128)S(1)} %bitcast.5) | data formatting | bytes 3145728
  61.6 0.6 copy.9
Async XLA Ops:
  0.6 1.4 %copy-start = (f32[4,3,64,4,128]{4,3,2,1,0:T(4,128)S(1)}, f32[4,3,64,4,128]{4,3,2,1,0:T(4,128)}, u32[]{:S(2)}) copy-start(f32[4,3,64,4,128]{4,3,2,1,0:T(4,128)} %param.4) | copy-start | bytes 4718596
  2.0 1.1 %copy-start.1 = (f32[2,3,64,4,128]{4,3,2,1,0:T(4,128)S(1)}, f32[2,3,64,4,128]{4,3,2,1,0:T(4,128)}, u32[]{:S(2)}) copy-start(f32[2,3,64,4,128]{4,3,2,1,0:T(4,128)} %param.5) | copy-start | bytes 2359300

commit v2 on v1

v2 whole, which is shorter than its diff:
```python
import functools
import math

import jax
import jax.numpy as jnp
from jax import lax
from jax.experimental import pallas as pl
from jax.experimental.pallas import tpu as pltpu
from jax.sharding import PartitionSpec as P

MESH = pl.DeviceIdType.MESH
F32 = jnp.float32
STEP = 0.1
VISC = 0.2
V, C, M = 4, 3, 8
XL, LN = 4, 128
CHIPS_X = 4
PAIRS_C = 32
PAIRS_FF = 32
PAIRS_UF = 42
PAIRS_UU = 74
PAIRS = 110


def kernel(
    n_gx, n_gy, nz, cells,
    q_hbm, b_hbm, d_hbm, u_hbm, out, growth_ref,
    q, b, d, u, a1, q1, f, terms, part,
    xs, xr, bxs, bxr, ys, yr, bys, byr, w, wb,
    acc, ca, cb, coef, g1, g2,
    in_sem, sx_sem, rx_sem, sy_sem, ry_sem, sg_sem, rg_sem, known,
):
    rows = nz * XL
    blocks = nz // 8
    nf = V * C
    gx, gy = lax.axis_index("gx"), lax.axis_index("gy")
    core = lax.rem(gx, 2)
    cx = lax.rem(lax.div(gx, 2), CHIPS_X)
    cz = lax.div(gx, 2 * CHIPS_X)
    n_z = n_gx // (2 * CHIPS_X)
    size_a, size_b = 2 * n_z, CHIPS_X * n_gy
    me_a, me_b = cz * 2 + core, cx * n_gy + gy

    def ring(size):
        return sorted(range(1, size), key=lambda s: -min(s, size - s)) + [0]

    zs = [lax.rem(cz + s, n_z) if s else cz for s in ring(n_z)]
    peers_a = [
        ((z * CHIPS_X + cx) * 2 + c, gy) for z in zs for c in (1 - core, core)
    ][: size_a - 1]
    xs_, ys_ = (
        [lax.rem(cx + s, CHIPS_X) if s else cx for s in ring(CHIPS_X)],
        [lax.rem(gy + s, n_gy) if s else gy for s in ring(n_gy)],
    )
    peers_b = [((cz * CHIPS_X + x) * 2 + core, y) for x in xs_ for y in ys_][: size_b - 1]

    def hops(size, n):
        s = (ring(size))[n]
        return min(s, size - s)

    order = sorted(
        (
            (i, j, k, n)
            for i in range(n_z) for j in range(CHIPS_X) for k in range(n_gy) for n in range(2)
        ),
        key=lambda t: -(4 * (hops(n_z, t[0]) + hops(CHIPS_X, t[1]) + hops(n_gy, t[2])) + (t[3] == 0)),
    )[:-1]
    peers_all = [
        ((zs[i] * CHIPS_X + xs_[j]) * 2 + (1 - core if n == 0 else core), ys_[k]) for i, j, k, n in order
    ]

    left, right = (lax.rem(gx + n_gx - 1, n_gx), gy), (lax.rem(gx + 1, n_gx), gy)
    below, above = (gx, lax.rem(gy + n_gy - 1, n_gy)), (gx, lax.rem(gy + 1, n_gy))
    has_l, has_r = gx > 0, gx < n_gx - 1
    has_b, has_a = gy > 0, gy < n_gy - 1

    def total_of(terms):
        terms = list(terms)
        while len(terms) > 1:
            terms = [
                terms[i] + terms[i + 1] if i + 1 < len(terms) else terms[i] for i in range(0, len(terms), 2)
            ]
        return terms[0]

    q_main = pltpu.make_async_copy(q_hbm, q.at[:, pl.ds(8, rows), :], in_sem.at[0])
    q_low = pltpu.make_async_copy(q_hbm.at[:, pl.ds(rows - 8, 8), :], q.at[:, pl.ds(0, 8), :], in_sem.at[1])
    q_high = pltpu.make_async_copy(q_hbm.at[:, pl.ds(0, 8), :], q.at[:, pl.ds(rows + 8, 8), :], in_sem.at[2])
    b_main = pltpu.make_async_copy(b_hbm, b.at[:, pl.ds(8, rows), :], in_sem.at[3])
    b_low = pltpu.make_async_copy(b_hbm.at[:, pl.ds(rows - 8, 8), :], b.at[:, pl.ds(0, 8), :], in_sem.at[4])
    b_high = pltpu.make_async_copy(b_hbm.at[:, pl.ds(0, 8), :], b.at[:, pl.ds(rows + 8, 8), :], in_sem.at[5])
    u_main = pltpu.make_async_copy(u_hbm, u, in_sem.at[6])
    d_main = pltpu.make_async_copy(d_hbm, d, in_sem.at[7])
    q_main.start()
    b_main.start()
    for copy in (q_low, q_high, b_low, b_high, u_main, d_main):
        copy.start()

    barrier = pltpu.get_barrier_semaphore()
    for peer in (left, right, below, above):
        pl.semaphore_signal(barrier, inc=1, device_id=peer, device_id_type=MESH)

    for peer in peers_a + peers_b:
        pl.semaphore_signal(barrier, inc=1, device_id=peer, device_id_type=MESH)

    lane = lax.broadcasted_iota(jnp.int32, (8, LN), 1)
    half = lax.shift_right_logical(lane, 1)
    first, final, odd = lane == 0, lane == LN - 1, lax.rem(lane, 2) == 1

    def plane(ref, field, k, x, dz=0, pad=8):
        return ref[field, pl.ds(pad + 8 * XL * k + x + XL * dz, 8, stride=XL), :]

    def zero(ref, count):
        @pl.loop(0, count)
        def _(i):
            ref[i] = jnp.zeros((nz, LN), F32)

    def x_copy(send, recv, fields, side, sem):
        peer = left if side == 0 else right
        return pltpu.make_async_remote_copy(
            src_ref=send.at[side, fields], dst_ref=recv.at[1 - side, fields],
            send_sem=sx_sem.at[sem + side], recv_sem=rx_sem.at[sem + 1 - side],
            device_id=peer, device_id_type=MESH,
        )

    def x_each(act):
        for side, there in ((0, has_l), (1, has_r)):
            @pl.when(there)
            def _():
                act(side)

    def x_start(send, recv, fields, sem):
        x_each(lambda side: x_copy(send, recv, fields, side, sem).start())

    def x_wait(send, recv, fields, sem):
        x_each(lambda side: x_copy(send, recv, fields, 1 - side, sem).wait_recv())

    def x_sent(send, recv, fields, sem):
        x_each(lambda side: x_copy(send, recv, fields, side, sem).wait_send())

    def x_zero(recv, count):
        for side, there in ((0, has_l), (1, has_r)):
            @pl.when(jnp.logical_not(there))
            def _():
                zero(recv.at[side], count)

    def y_copy(send, recv, side, sem):
        peer = below if side == 0 else above
        return pltpu.make_async_remote_copy(
            src_ref=send, dst_ref=recv.at[1 - side],
            send_sem=sy_sem.at[sem + side], recv_sem=ry_sem.at[sem + 1 - side],
            device_id=peer, device_id_type=MESH,
        )

    def y_start(send, recv, sem):
        for side, there in ((0, has_b), (1, has_a)):
            @pl.when(there)
            def _():
                y_copy(send, recv, side, sem).start()

    def y_wait(send, recv, sem):
        for side, there in ((0, has_b), (1, has_a)):
            @pl.when(there)
            def _():
                y_copy(send, recv, 1 - side, sem).wait_recv()

    def y_sent(send, recv, sem):
        for side, there in ((0, has_b), (1, has_a)):
            @pl.when(there)
            def _():
                y_copy(send, recv, side, sem).wait_send()

    def y_zero(recv):
        for side, there in ((0, has_b), (1, has_a)):
            @pl.when(jnp.logical_not(there))
            def _():
                recv[side] = jnp.zeros((nz, LN), F32)

    def x_pack(ref, send, count):
        @pl.loop(0, count)
        def _(i):
            for k in range(blocks):
                at = pl.ds(8 * k, 8)
                send[0, i, at, :] = plane(ref, i, k, 0)
                send[1, i, at, :] = plane(ref, i, k, XL - 1)

    def y_pack(ref, send, count):
        @pl.loop(0, blocks)
        def _(k):
            total = jnp.zeros((8, LN), F32)
            for x in range(XL):
                for i in range(count):
                    at = 16 * x + i
                    total = jnp.where(half == at, pltpu.roll(plane(ref, i, k, x), 2 * at + 1, 1), total)
            send[pl.ds(pl.multiple_of(8 * k, 8), 8), :] = total

    def y_merge(recv, merged):
        for k in range(blocks):
            at = pl.ds(8 * k, 8)
            merged[at, :] = jnp.where(
                odd, pltpu.roll(recv[0, at, :], 1, 1), pltpu.roll(recv[1, at, :], LN - 1, 1)
            )

    def beside_y(value, edges, x, field):
        fix = pltpu.roll(edges, LN - (32 * x + 2 * field + 1), 1)
        return (
            jnp.where(first, fix, pltpu.roll(value, 1, 1)),
            jnp.where(final, fix, pltpu.roll(value, LN - 1, 1)),
        )

    def beside_x(ref, recv, field, k, x):
        at = pl.ds(pl.multiple_of(8 * k, 8), 8)
        low = recv[0, field, at, :] if x == 0 else plane(ref, field, k, x - 1)
        high = recv[1, field, at, :] if x == XL - 1 else plane(ref, field, k, x + 1)
        return low, high

    def base_terms(s, planes):
        @pl.loop(0, blocks)
        def _(k):
            wbk = wb[pl.ds(pl.multiple_of(8 * k, 8), 8), :]
            for x in planes:
                at = pl.ds(pl.multiple_of(8 * k, 8) + nz * x, 8)
                mix = [[None] * C for _ in range(C)]
                for j in range(C):
                    field = 3 * s + j
                    mid = plane(b, field, k, x)
                    xm, xp = beside_x(b, bxr, field, k, x)
                    ym, yp = beside_y(mid, wbk, x, field)
                    zm, zp = plane(b, field, k, x, -1), plane(b, field, k, x, 1)
                    for c, (m_, p_) in enumerate(((xm, xp), (ym, yp), (zm, zp))):
                        mix[c][j] = 0.5 * STEP * (m_ - p_)
                    terms[s, 2 * j, at, :] = VISC * STEP - 0.5 * STEP * mid
                    terms[s, 2 * j + 1, at, :] = VISC * STEP + 0.5 * STEP * mid
                for c in range(C):
                    for j in range(C):
                        extra = 1.0 - 6.0 * VISC * STEP if c == j else 0.0
                        terms[s, 6 + C * c + j, at, :] = mix[c][j] + extra if extra else mix[c][j]

    def stencil(src, src_x, edges, s, dst, planes, vectors):
        @pl.loop(0, blocks)
        def _(k):
            wk = edges[pl.ds(pl.multiple_of(8 * k, 8), 8), :]
            for x in planes:
                at = pl.ds(pl.multiple_of(8 * k, 8) + nz * x, 8)
                side = [terms[s, n, at, :] for n in range(6)]
                mix = [[terms[s, 6 + C * c + j, at, :] for j in range(C)] for c in range(C)]
                for v in vectors:
                    mid = [plane(src, C * v + c, k, x) for c in range(C)]
                    for c in range(C):
                        field = C * v + c
                        xm, xp = beside_x(src, src_x, field, k, x)
                        ym, yp = beside_y(mid[c], wk, x, field)
                        zm, zp = plane(src, field, k, x, -1), plane(src, field, k, x, 1)
                        total = mix[c][0] * mid[0] + mix[c][1] * mid[1] + mix[c][2] * mid[2]
                        total = total + (side[0] * xm + side[1] * xp)
                        total = total + (side[2] * ym + side[3] * yp)
                        total = total + (side[4] * zm + side[5] * zp)
                        dst[field, pl.ds(8 * XL * k + x, 8, stride=XL), :] = total

    def pair_sums(pairs, loader, planes, fresh):
        def body(k, sums):
            sums = list(sums)
            for x in planes:
                at = pl.ds(8 * XL * k + x, 8, stride=XL)
                for c in range(C):
                    left_, right_ = loader(c, at)
                    for n, (_, i, j) in enumerate(pairs):
                        sums[n] = sums[n] + left_[i] * right_[j]
            return tuple(sums)

        begin = tuple(jnp.zeros((8, LN), F32) if fresh else part[n] for n, _, _ in pairs)
        for (n, _, _), value in zip(pairs, lax.fori_loop(0, blocks, body, begin)):
            part[n] = value

    def on_modes(vectors, field):
        pairs = [(V * m + i, m, n) for n, i in enumerate(vectors) for m in range(M)]

        def loader(c, at):
            return [d[C * m + c, at, :] for m in range(M)], [field[C * i + c, at, :] for i in vectors]

        return pairs, loader

    tri = [(i, j) for i in range(V) for j in range(i, V)]
    uu = [(i, j) for i in range(M) for j in range(i, M)]

    def on_duals(vectors, field):
        count = vectors[-1] + 1
        pairs = [(PAIRS_FF + n, M + i, j) for n, (i, j) in enumerate(tri) if j in vectors]
        pairs += [(PAIRS_UF + V * m + i, m, i) for m in range(M) for i in vectors]

        def loader(c, at):
            fs = [field[C * i + c, at, :] for i in range(count)]
            return [u[C * m + c, at, :] for m in range(M)] + fs, fs

        return pairs, loader

    def among_duals():
        def loader(c, at):
            both = [u[C * m + c, at, :] for m in range(M)]
            return both, both

        return [(PAIRS_UU + n, i, j) for n, (i, j) in enumerate(uu)], loader

    def fold(start, count):
        for n in range(start, start + count):
            acc[pl.ds(n, 1), :] = jnp.sum(part[n], axis=0, keepdims=True)

    ones = jnp.ones((8, LN), F32)

    def all_reduce(buf, row, sem, fill=None):
        me = gx * n_gy + gy
        size = n_gx * n_gy
        buf[me] = row

        def copy(rows_, peer):
            return pltpu.make_async_remote_copy(
                src_ref=buf.at[rows_], dst_ref=buf.at[rows_],
                send_sem=sg_sem.at[sem], recv_sem=rg_sem.at[sem],
                device_id=peer, device_id_type=MESH,
            )

        for peer in peers_all:
            copy(me, peer).start()
        if fill is not None:
            fill()
        copy(pl.ds(0, size - 1), peers_all[0]).wait_recv()
        sums = total_of([total_of(buf[i + k] for k in range(16)) for i in range(0, size, 16)])
        return sums, copy(pl.ds(0, size - 1), peers_all[0])

    def lane_sums():
        return lax.dot_general(
            ones, acc[...], (((1,), (1,)), ((), ())),
            precision=lax.Precision.HIGHEST, preferred_element_type=F32,
        )[0:1, :]

    def spread(row, count, dst):
        r = lax.broadcasted_iota(jnp.int32, (count, LN), 0)
        l = lax.broadcasted_iota(jnp.int32, (count, LN), 1)
        chosen = jnp.where(r == l, jnp.broadcast_to(row, (count, LN)), 0.0)
        dst[pl.ds(0, count), :] = lax.dot_general(
            chosen, jnp.ones((LN, LN), F32), (((1,), (0,)), ((), ())),
            precision=lax.Precision.HIGHEST, preferred_element_type=F32,
        )

    everything = (1, 2, 0, 3)
    inner, outer = (1, 2), (0, 3)
    chunks = ((0, 1), (2, 3))
    fields_of = [pl.ds(C * c[0], C * len(c)) for c in chunks]
    snapshot = [pl.ds(C * s, C) for s in range(2)]
    q_main.wait()
    x_pack(q, xs.at[0], nf)
    b_main.wait()
    x_pack(b, bxs, 2 * C)
    pl.semaphore_wait(barrier, 4 + len(peers_a) + len(peers_b))
    x_start(bxs, bxr, snapshot[0], 0)
    for n, fields in enumerate(fields_of):
        x_start(xs.at[0], xr.at[0], fields, 4 + 2 * n)
    x_start(bxs, bxr, snapshot[1], 2)
    for peer in peers_a:
        pl.semaphore_signal(known, inc=1, device_id=peer, device_id_type=MESH)
    y_pack(b, bys, 2 * C)
    y_start(bys, byr, 2)
    y_pack(q, ys.at[0], nf)
    y_start(ys.at[0], yr.at[0], 0)
    acc[...] = jnp.zeros((LN, LN), F32)
    x_zero(xr.at[0], nf)
    x_zero(xr.at[1], nf)
    x_zero(bxr, 2 * C)
    y_zero(yr.at[0])
    y_zero(yr.at[1])
    y_zero(byr)
    for copy in (q_low, q_high, b_low, b_high):
        copy.wait()
    y_wait(bys, byr, 2)
    y_merge(byr, wb)
    base_terms(0, inner)
    y_wait(ys.at[0], yr.at[0], 0)
    y_merge(yr.at[0], w)
    stencil(q, xr.at[0], w, 0, a1, inner, range(V))
    d_main.wait()

    pair_sums(*on_modes(tuple(range(V)), a1), inner, True)
    x_wait(bxs, bxr, snapshot[0], 0)
    base_terms(0, outer)
    for n, fields in enumerate(fields_of):
        x_wait(xs.at[0], xr.at[0], fields, 4 + 2 * n)
        stencil(q, xr.at[0], w, 0, a1, outer, chunks[n])
    pair_sums(*on_modes(tuple(range(V)), a1), outer, False)
    fold(0, PAIRS_C)

    def second_base():
        x_wait(bxs, bxr, snapshot[1], 2)
        base_terms(1, everything)

    def dual_products():
        u_main.wait()
        pair_sums(*among_duals(), everything, True)

    def shadow():
        second_base()
        dual_products()

    pl.semaphore_wait(known, len(peers_a))
    row1, sent1 = all_reduce(g1, lane_sums(), 0, shadow)
    fold(PAIRS_UU, len(uu))
    spread(row1, PAIRS_C, ca)

    def deflate(planes, vectors, send):
        weight = {
            (m, i): jnp.broadcast_to(ca[pl.ds(V * m + i, 1), :], (8, LN)) for m in range(M) for i in vectors
        }

        @pl.loop(0, blocks)
        def _(k):
            at = pl.ds(pl.multiple_of(8 * k, 8), 8)
            for c in range(C):
                for x in planes:
                    dual = [plane(u, C * m + c, k, x, 0, 0) for m in range(M)]
                    for i in vectors:
                        field = C * i + c
                        total = plane(a1, field, k, x, 0, 0) - total_of(weight[m, i] * dual[m] for m in range(M))
                        q1[field, pl.ds(8 + 8 * XL * k + x, 8, stride=XL), :] = total
                        if send:
                            xs[1, 0 if x == 0 else 1, field, at, :] = total

    for n, fields in enumerate(fields_of):
        deflate(outer, chunks[n], True)
        x_start(xs.at[1], xr.at[1], fields, 12 + 2 * n)
    deflate(inner, range(V), False)
    y_pack(q1, ys.at[1], nf)
    y_start(ys.at[1], yr.at[1], 4)
    for field in range(nf):
        q1[field, pl.ds(0, 8), :] = q1[field, pl.ds(rows, 8), :]
        q1[field, pl.ds(rows + 8, 8), :] = q1[field, pl.ds(8, 8), :]
    y_wait(ys.at[1], yr.at[1], 4)
    y_merge(yr.at[1], w)
    stencil(q1, xr.at[1], w, 1, f, inner, range(V))

    pair_sums(*on_modes(tuple(range(V)), f), inner, True)
    pair_sums(*on_duals(tuple(range(V)), f), inner, True)
    for n, fields in enumerate(fields_of):
        x_wait(xs.at[1], xr.at[1], fields, 12 + 2 * n)
        stencil(q1, xr.at[1], w, 1, f, outer, chunks[n])
    pair_sums(*on_modes(tuple(range(V)), f), outer, False)
    pair_sums(*on_duals(tuple(range(V)), f), outer, False)
    fold(0, PAIRS_UU)
    row2, sent2 = all_reduce(g2, lane_sums(), 1)
    spread(row2, 112, cb)

    def val(n):
        return cb[pl.ds(n, 1), :]

    c2 = [[val(V * m + i) for i in range(V)] for m in range(M)]
    ff, uf, dd = {}, {}, {}
    for n, (i, j) in enumerate(tri):
        ff[i, j] = val(PAIRS_FF + n)
    for m in range(M):
        for i in range(V):
            uf[m, i] = val(PAIRS_UF + V * m + i)
    for n, (i, j) in enumerate(uu):
        dd[i, j] = dd[j, i] = val(PAIRS_UU + n)

    gram = {}
    for j in range(V):
        h = [total_of(dd[m, n] * c2[n][j] for n in range(M)) - uf[m, j] for m in range(M)]
        for i in range(j, V):
            gram[i, j] = ff[j, i] + total_of(c2[m][i] * h[m] - c2[m][j] * uf[m, i] for m in range(M))
    low = {}
    inv = {}
    for j in range(V):
        pivot = gram[j, j]
        for k in range(j):
            pivot = pivot - low[j, k] * low[j, k]
        low[j, j] = jnp.sqrt(pivot)
        inv[j, j] = 1.0 / low[j, j]
        for i in range(j + 1, V):
            total = gram[i, j]
            for k in range(j):
                total = total - low[i, k] * low[j, k]
            low[i, j] = total * inv[j, j]
    for i in range(V):
        for j in range(i):
            total = low[i, j] * inv[j, j]
            for k in range(j + 1, i):
                total = total + low[i, k] * inv[k, j]
            inv[i, j] = -total * inv[i, i]
    lane1 = lax.broadcasted_iota(jnp.int32, (1, LN), 1)
    for i in range(V):
        row = jnp.zeros((1, LN), F32)
        for j in range(i + 1):
            row = jnp.where(lane1 == j, low[i, j], row)
        growth_ref[pl.ds(i, 1), :] = row[:, 0:V]
    scale = math.sqrt(cells)
    slot = {}
    n = 0
    for i in range(V):
        for j in range(i + 1):
            coef[pl.ds(n, 1), :] = scale * inv[i, j]
            slot["f", i, j] = n
            n += 1
    for i in range(V):
        for m in range(M):
            coef[pl.ds(n, 1), :] = -scale * total_of(inv[i, j] * c2[m][j] for j in range(i + 1))
            slot["u", i, m] = n
            n += 1

    for pick in ((0, 1), (2, 3)):
        weight = {
            key: jnp.broadcast_to(coef[pl.ds(n, 1), :], (8, LN)) for key, n in slot.items() if key[1] in pick
        }

        @pl.loop(0, rows // 8)
        def _(t):
            at = pl.ds(pl.multiple_of(8 * t, 8), 8)
            for c in range(C):
                fs = [f[C * i + c, at, :] for i in range(pick[-1] + 1)]
                us = [u[C * m + c, at, :] for m in range(M)]
                for i in pick:
                    terms = [weight["f", i, j] * fs[j] for j in range(i + 1)]
                    terms += [weight["u", i, m] * us[m] for m in range(M)]
                    out[C * i + c, at, :] = total_of(terms)

    for n in range(2):
        x_sent(bxs, bxr, snapshot[n], 2 * n)
    for n in range(2):
        x_sent(xs.at[0], xr.at[0], fields_of[n], 4 + 2 * n)
        x_sent(xs.at[1], xr.at[1], fields_of[n], 12 + 2 * n)
    sent1.wait_send()
    sent2.wait_send()
    y_sent(ys.at[0], yr.at[0], 0)
    y_sent(bys, byr, 2)
    y_sent(ys.at[1], yr.at[1], 4)


def body(n_gx, n_gy, adjoint_block, base_flow, direct_modes, dual_modes):
    nz = adjoint_block.shape[2]
    rows = nz * XL
    cells = float(C * nz * XL * n_gx * LN * n_gy)
    nf = V * C
    vm = lambda *shape: pltpu.VMEM(shape, F32)
    in_hbm = lambda array: pltpu.with_memory_space_constraint(array, pltpu.HBM)
    anyspace = pl.BlockSpec(memory_space=pltpu.HBM)
    out, growth = pl.pallas_call(
        functools.partial(kernel, n_gx, n_gy, nz, cells),
        name="adjoint_step",
        out_shape=(
            jax.ShapeDtypeStruct((nf, rows, LN), F32),
            jax.ShapeDtypeStruct((V, V), F32),
        ),
        in_specs=[anyspace] * 4,
        out_specs=(pl.BlockSpec(memory_space=pltpu.VMEM),) * 2,
        scratch_shapes=[
            vm(nf, rows + 16, LN), vm(2 * C, rows + 16, LN), vm(M * C, rows, LN), vm(M * C, rows, LN),
            vm(nf, rows, LN), vm(nf, rows + 16, LN), vm(nf, rows, LN),
            vm(2, 15, rows, LN), vm(PAIRS, 8, LN),
            vm(2, 2, nf, nz, LN), vm(2, 2, nf, nz, LN), vm(2, 2 * C, nz, LN), vm(2, 2 * C, nz, LN),
            vm(2, nz, LN), vm(2, 2, nz, LN), vm(nz, LN), vm(2, nz, LN), vm(nz, LN), vm(nz, LN),
            vm(LN, LN), vm(PAIRS_C, LN), vm(112, LN), vm(48, LN),
            vm(n_gx * n_gy, 1, LN), vm(n_gx * n_gy, 1, LN),
            pltpu.SemaphoreType.DMA((8,)),
            pltpu.SemaphoreType.DMA((20,)), pltpu.SemaphoreType.DMA((20,)),
            pltpu.SemaphoreType.DMA((6,)), pltpu.SemaphoreType.DMA((6,)),
            pltpu.SemaphoreType.DMA((2,)), pltpu.SemaphoreType.DMA((2,)), pltpu.SemaphoreType.REGULAR,
        ],
        compiler_params=pltpu.CompilerParams(
            collective_id=0, has_side_effects=True, vmem_limit_bytes=48 * 1024 * 1024
        ),
    )(
        in_hbm(adjoint_block.reshape(nf, rows, LN)),
        in_hbm(base_flow.reshape(2 * C, rows, LN)),
        in_hbm(direct_modes.reshape(M * C, rows, LN)),
        in_hbm(dual_modes.reshape(M * C, rows, LN)),
    )
    return out.reshape(adjoint_block.shape), growth


def solution(mesh):
    spec = P(None, None, None, "gx", "gy")
    return jax.shard_map(
        functools.partial(body, mesh.shape["gx"], mesh.shape["gy"]),
        mesh=mesh,
        in_specs=(spec,) * 4,
        out_specs=(spec, P()),
        check_vma=False,
    )
```

time: 62.3 us -> 51.2 us (0.82)
  Pallas kernels: 57.2 us -> 48.7 us
  local copies, waits for them, and re-layouts: 4.26 us -> 1.72 us
    pallas_call x1, Pallas kernels: 57.2 us -> 48.7 us  [body(): pl.pallas_call(functools.partial(kernel, n_gx, n_gy, nz, cells), name='ad...]
    unnamed x6 -> x2, local copies, waits for them, and re-layouts: 4.26 us -> 1.72 us
where the time goes in v2:
time: 51.2 us; the launch traced here: 51.1 us
  Pallas kernels  48.7 us (95%)
  local copies, waits for them, and re-layouts  1.72 us (3%)
  between operations  0.64 us (1%)
    pallas_call x1, Pallas kernels, body(): pl.pallas_call(functools.partial(kernel, n_gx, n_gy, nz, cells), name='ad...  48.7 us
    unnamed x2, local copies, waits for them, and re-layouts  1.72 us

profile of v2, /device:TPU:1, one launch (start us, length us, event | category | flops | bytes accessed | tf_op | source)
XLA Modules:
  0.0 51.1 jit_solution(2072940749738265830)
XLA Ops:
  0.6 48.7 %adjoint_step.1 = (f32[12,256,128]{2,1,0:T(8,128)S(1)}, f32[4,4]{1,0:T(4,128)S(1)}) custom-call(f32[12,256,128]{2,1,0:T(8,128)} %bitcast.8, f32[6,256,128]{2,1,0:T(8,128)} %bitcast.9, f32[24,256,128]{2,1,0:T(8,128)} %bitcast.6, f32[24,256,128]{2,1,0:T(8,128)} %bitcast.7), custom_call_target="tpu_custom_call" | custom-call | tf_op jit(solution)/shard_map/adjoint_step/pallas_call | solution.py:542
  49.4 1.1 %copy.8 = f32[4,3,64,4,128]{4,3,2,1,0:T(4,128)} copy(f32[4,3,64,4,128]{4,3,2,1,0:T(4,128)S(1)} %bitcast.5) | data formatting | bytes 3145728
  50.5 0.6 %copy.9 = f32[4,4]{1,0:T(4,128)} copy(f32[4,4]{1,0:T(4,128)S(1)} %get-tuple-element.9) | data formatting | bytes 128

commit v3 on v2

--- a/solution.py
+++ b/solution.py
@@ -38,21 +38,19 @@
     cx = lax.rem(lax.div(gx, 2), CHIPS_X)
     cz = lax.div(gx, 2 * CHIPS_X)
     n_z = n_gx // (2 * CHIPS_X)
-    size_a, size_b = 2 * n_z, CHIPS_X * n_gy
-    me_a, me_b = cz * 2 + core, cx * n_gy + gy
 
     def ring(size):
         return sorted(range(1, size), key=lambda s: -min(s, size - s)) + [0]
 
     zs = [lax.rem(cz + s, n_z) if s else cz for s in ring(n_z)]
-    peers_a = [
-        ((z * CHIPS_X + cx) * 2 + c, gy) for z in zs for c in (1 - core, core)
-    ][: size_a - 1]
-    xs_, ys_ = (
-        [lax.rem(cx + s, CHIPS_X) if s else cx for s in ring(CHIPS_X)],
-        [lax.rem(gy + s, n_gy) if s else gy for s in ring(n_gy)],
-    )
-    peers_b = [((cz * CHIPS_X + x) * 2 + core, y) for x in xs_ for y in ys_][: size_b - 1]
+    xs_ = [lax.rem(cx + s, CHIPS_X) if s else cx for s in ring(CHIPS_X)]
+    ys_ = [lax.rem(gy + s, n_gy) if s else gy for s in ring(n_gy)]
+    peers_z = [((z * CHIPS_X + cx) * 2 + c, gy) for z in zs for c in (1 - core, core)][:-1]
+    peers_x = [((cz * CHIPS_X + x) * 2 + core, gy) for x in xs_][:-1]
+    peers_y = [(gx, y) for y in ys_][:-1]
+    peers_near = [
+        p for s, p in zip([s for s in ring(n_z) for _ in range(2)], peers_z) if min(s, n_z - s) <= max(n_z // 4, 1)
+    ]
 
     def hops(size, n):
         s = (ring(size))[n]
@@ -99,7 +97,7 @@
     for peer in (left, right, below, above):
         pl.semaphore_signal(barrier, inc=1, device_id=peer, device_id_type=MESH)
 
-    for peer in peers_a + peers_b:
+    for peer in peers_x + peers_y + peers_near:
         pl.semaphore_signal(barrier, inc=1, device_id=peer, device_id_type=MESH)
 
     lane = lax.broadcasted_iota(jnp.int32, (8, LN), 1)
@@ -347,16 +345,16 @@
     fields_of = [pl.ds(C * c[0], C * len(c)) for c in chunks]
     snapshot = [pl.ds(C * s, C) for s in range(2)]
     q_main.wait()
+    b_main.wait()
     x_pack(q, xs.at[0], nf)
-    b_main.wait()
     x_pack(b, bxs, 2 * C)
-    pl.semaphore_wait(barrier, 4 + len(peers_a) + len(peers_b))
+    pl.semaphore_wait(barrier, 4 + len(peers_x) + len(peers_y) + len(peers_near))
     x_start(bxs, bxr, snapshot[0], 0)
     for n, fields in enumerate(fields_of):
         x_start(xs.at[0], xr.at[0], fields, 4 + 2 * n)
     x_start(bxs, bxr, snapshot[1], 2)
-    for peer in peers_a:
-        pl.semaphore_signal(known, inc=1, device_id=peer, device_id_type=MESH)
+    for peer in peers_x + peers_near:
+        pl.semaphore_signal(known.at[0], inc=1, device_id=peer, device_id_type=MESH)
     y_pack(b, bys, 2 * C)
     y_start(bys, byr, 2)
     y_pack(q, ys.at[0], nf)
@@ -376,6 +374,9 @@
     y_wait(ys.at[0], yr.at[0], 0)
     y_merge(yr.at[0], w)
     stencil(q, xr.at[0], w, 0, a1, inner, range(V))
+    pl.semaphore_wait(known.at[0], len(peers_x) + len(peers_near))
+    for peer in peers_z:
+        pl.semaphore_signal(known.at[1], inc=1, device_id=peer, device_id_type=MESH)
     d_main.wait()
 
     pair_sums(*on_modes(tuple(range(V)), a1), inner, True)
@@ -384,7 +385,7 @@
     for n, fields in enumerate(fields_of):
         x_wait(xs.at[0], xr.at[0], fields, 4 + 2 * n)
         stencil(q, xr.at[0], w, 0, a1, outer, chunks[n])
-    pair_sums(*on_modes(tuple(range(V)), a1), outer, False)
+        pair_sums(*on_modes(chunks[n], a1), outer, False)
     fold(0, PAIRS_C)
 
     def second_base():
@@ -399,7 +400,7 @@
         second_base()
         dual_products()
 
-    pl.semaphore_wait(known, len(peers_a))
+    pl.semaphore_wait(known.at[1], len(peers_z))
     row1, sent1 = all_reduce(g1, lane_sums(), 0, shadow)
     fold(PAIRS_UU, len(uu))
     spread(row1, PAIRS_C, ca)
@@ -440,8 +441,8 @@
     for n, fields in enumerate(fields_of):
         x_wait(xs.at[1], xr.at[1], fields, 12 + 2 * n)
         stencil(q1, xr.at[1], w, 1, f, outer, chunks[n])
-    pair_sums(*on_modes(tuple(range(V)), f), outer, False)
-    pair_sums(*on_duals(tuple(range(V)), f), outer, False)
+        pair_sums(*on_modes(chunks[n], f), outer, False)
+        pair_sums(*on_duals(chunks[n], f), outer, False)
     fold(0, PAIRS_UU)
     row2, sent2 = all_reduce(g2, lane_sums(), 1)
     spread(row2, 112, cb)
@@ -559,7 +560,7 @@
             pltpu.SemaphoreType.DMA((8,)),
             pltpu.SemaphoreType.DMA((20,)), pltpu.SemaphoreType.DMA((20,)),
             pltpu.SemaphoreType.DMA((6,)), pltpu.SemaphoreType.DMA((6,)),
-            pltpu.SemaphoreType.DMA((2,)), pltpu.SemaphoreType.DMA((2,)), pltpu.SemaphoreType.REGULAR,
+            pltpu.SemaphoreType.DMA((2,)), pltpu.SemaphoreType.DMA((2,)), pltpu.SemaphoreType.REGULAR((2,)),
         ],
         compiler_params=pltpu.CompilerParams(
             collective_id=0, has_side_effects=True, vmem_limit_bytes=48 * 1024 * 1024

time: 51.2 us -> 50.3 us (0.982)
  Pallas kernels: 48.7 us -> 47.9 us
    pallas_call x1, Pallas kernels: 48.7 us -> 47.9 us  [body(): pl.pallas_call(functools.partial(kernel, n_gx, n_gy, nz, cells), name='ad...]
where the time goes in v3:
time: 50.3 us; the launch traced here: 50.2 us
  Pallas kernels  47.9 us (95%)
  local copies, waits for them, and re-layouts  1.72 us (3%)
  between operations  0.64 us (1%)
    pallas_call x1, Pallas kernels, body(): pl.pallas_call(functools.partial(kernel, n_gx, n_gy, nz, cells), name='ad...  47.9 us
    unnamed x2, local copies, waits for them, and re-layouts  1.72 us

profile of v3, /device:TPU:1, one launch (start us, length us, event | category | flops | bytes accessed | tf_op | source)
XLA Modules:
  0.0 50.2 jit_solution(13421118817989497352)
XLA Ops:
  0.6 47.9 %adjoint_step.1 = (f32[12,256,128]{2,1,0:T(8,128)S(1)}, f32[4,4]{1,0:T(4,128)S(1)}) custom-call(f32[12,256,128]{2,1,0:T(8,128)} %bitcast.8, f32[6,256,128]{2,1,0:T(8,128)} %bitcast.9, f32[24,256,128]{2,1,0:T(8,128)} %bitcast.6, f32[24,256,128]{2,1,0:T(8,128)} %bitcast.7), custom_call_target="tpu_custom_call" | custom-call | tf_op jit(solution)/shard_map/adjoint_step/pallas_call | solution.py:543
  48.5 1.1 %copy.8 = f32[4,3,64,4,128]{4,3,2,1,0:T(4,128)} copy(f32[4,3,64,4,128]{4,3,2,1,0:T(4,128)S(1)} %bitcast.5) | data formatting | bytes 3145728
  49.7 0.6 %copy.9 = f32[4,4]{1,0:T(4,128)} copy(f32[4,4]{1,0:T(4,128)S(1)} %get-tuple-element.9) | data formatting | bytes 128

commit v4 on v3

--- a/solution.py
+++ b/solution.py
@@ -302,8 +302,6 @@
         for n in range(start, start + count):
             acc[pl.ds(n, 1), :] = jnp.sum(part[n], axis=0, keepdims=True)
 
-    ones = jnp.ones((8, LN), F32)
-
     def all_reduce(buf, row, sem, fill=None):
         me = gx * n_gy + gy
         size = n_gx * n_gy
@@ -324,20 +322,17 @@
         sums = total_of([total_of(buf[i + k] for k in range(16)) for i in range(0, size, 16)])
         return sums, copy(pl.ds(0, size - 1), peers_all[0])
 
-    def lane_sums():
-        return lax.dot_general(
-            ones, acc[...], (((1,), (1,)), ((), ())),
-            precision=lax.Precision.HIGHEST, preferred_element_type=F32,
-        )[0:1, :]
+    def eye(count):
+        r = lax.broadcasted_iota(jnp.int32, (count, LN), 0)
+        return r == lax.broadcasted_iota(jnp.int32, (count, LN), 1)
+
+    def lane_sums(count):
+        sums = jnp.sum(acc[pl.ds(0, count), :], axis=1, keepdims=True)
+        return jnp.sum(jnp.where(eye(count), sums, 0.0), axis=0, keepdims=True)
 
     def spread(row, count, dst):
-        r = lax.broadcasted_iota(jnp.int32, (count, LN), 0)
-        l = lax.broadcasted_iota(jnp.int32, (count, LN), 1)
-        chosen = jnp.where(r == l, jnp.broadcast_to(row, (count, LN)), 0.0)
-        dst[pl.ds(0, count), :] = lax.dot_general(
-            chosen, jnp.ones((LN, LN), F32), (((1,), (0,)), ((), ())),
-            precision=lax.Precision.HIGHEST, preferred_element_type=F32,
-        )
+        chosen = jnp.where(eye(count), jnp.broadcast_to(row, (count, LN)), 0.0)
+        dst[pl.ds(0, count), :] = jnp.broadcast_to(jnp.sum(chosen, axis=1, keepdims=True), (count, LN))
 
     everything = (1, 2, 0, 3)
     inner, outer = (1, 2), (0, 3)
@@ -401,7 +396,7 @@
         dual_products()
 
     pl.semaphore_wait(known.at[1], len(peers_z))
-    row1, sent1 = all_reduce(g1, lane_sums(), 0, shadow)
+    row1, sent1 = all_reduce(g1, lane_sums(PAIRS_C), 0, shadow)
     fold(PAIRS_UU, len(uu))
     spread(row1, PAIRS_C, ca)
 
@@ -444,7 +439,7 @@
         pair_sums(*on_modes(chunks[n], f), outer, False)
         pair_sums(*on_duals(chunks[n], f), outer, False)
     fold(0, PAIRS_UU)
-    row2, sent2 = all_reduce(g2, lane_sums(), 1)
+    row2, sent2 = all_reduce(g2, lane_sums(112), 1)
     spread(row2, 112, cb)
 
     def val(n):

time: 50.3 us -> 49.7 us (0.988)
  Pallas kernels: 47.9 us -> 47.2 us
    pallas_call x1, Pallas kernels: 47.9 us -> 47.2 us  [body(): pl.pallas_call(functools.partial(kernel, n_gx, n_gy, nz, cells), name='ad...]
where the time goes in v4:
time: 49.7 us; the launch traced here: 49.6 us
  Pallas kernels  47.2 us (95%)
  local copies, waits for them, and re-layouts  1.72 us (3%)
  between operations  0.64 us (1%)
    pallas_call x1, Pallas kernels, body(): pl.pallas_call(functools.partial(kernel, n_gx, n_gy, nz, cells), name='ad...  47.2 us
    unnamed x2, local copies, waits for them, and re-layouts  1.72 us

profile of v4, /device:TPU:1, one launch (start us, length us, event | category | flops | bytes accessed | tf_op | source)
XLA Modules:
  0.0 49.6 jit_solution(4353688583636787618)
XLA Ops:
  0.6 47.2 %adjoint_step.1 = (f32[12,256,128]{2,1,0:T(8,128)S(1)}, f32[4,4]{1,0:T(4,128)S(1)}) custom-call(f32[12,256,128]{2,1,0:T(8,128)} %bitcast.8, f32[6,256,128]{2,1,0:T(8,128)} %bitcast.9, f32[24,256,128]{2,1,0:T(8,128)} %bitcast.6, f32[24,256,128]{2,1,0:T(8,128)} %bitcast.7), custom_call_target="tpu_custom_call" | custom-call | tf_op jit(solution)/shard_map/adjoint_step/pallas_call | solution.py:538
  47.9 1.1 %copy.8 = f32[4,3,64,4,128]{4,3,2,1,0:T(4,128)} copy(f32[4,3,64,4,128]{4,3,2,1,0:T(4,128)S(1)} %bitcast.5) | data formatting | bytes 3145728
  49.0 0.6 %copy.9 = f32[4,4]{1,0:T(4,128)} copy(f32[4,4]{1,0:T(4,128)S(1)} %get-tuple-element.9) | data formatting | bytes 128
